TPU v7x, 128 devices: a whole 4x4x4 slice. The times are simulated.
128 devices in a mesh: gz: 8 (over z, y_hi), gx: 16 (over x, y_lo, core).
Axes of the slice: x: 4, y: 4 (y_hi: 2, y_lo: 2; y = y_hi * 2 + y_lo), z: 4, core: 2. Of those that a mesh axis runs over, the one named last changes fastest.
Arguments:
- strain: float32 [6, 2, 1024, 1024], P(None, None, 'gx', 'gz'), may hold values from -6 to 6
- labels: int32 [2, 1024, 1024], P(None, 'gx', 'gz'), may hold values 0 or 1
- normals: int32 [2, 64, 64], P(None, 'gx', 'gz'), may hold values from 0 to 7
- moduli: float32 [5], replicated, may hold values from 0.5 to 4
- mean_strain: float32 [6], replicated, may hold values from -4 to 4
Outputs:
- strain_next: float32 [6, 2, 1024, 1024], P(None, None, 'gx', 'gz')
- stress_next: float32 [6, 2, 1024, 1024], P(None, None, 'gx', 'gz')
All inputs are finite; a program needn't handle non-finite values. No bound on the sum of `labels` on one device may be relied on, other than what follows from the above.
Results may differ from a plain program's by a relative error of at most 0.000082.
Values sent between devices are 32-bit elements; how exact they have to be, the bound alone decides.
A program may use at most 128 MiB of HBM per device.

v0:
```python
import functools
import math

import jax
import jax.numpy as jnp
import numpy as np
from jax import lax
from jax.experimental import pallas as pl
from jax.experimental.pallas import tpu as pltpu
from jax.sharding import PartitionSpec as P

ANGLES = 8
BLK = 16
COMPS = (0, 2, 4, 3, 5)
MESH = pl.DeviceIdType.MESH
HIGH = lax.Precision.HIGHEST
ROOT = math.sqrt(0.5)


def tables():
    k = np.arange(128)
    w = 2.0 * np.pi / 128.0 * (k[:, None] * k[None, :] % 128)
    dft = np.concatenate([np.cos(w), np.sin(w)], axis=1)
    r = np.arange(8)
    wz = 2.0 * np.pi / 1024.0 * (r[:, None] * k[None, :])
    twz = np.concatenate([np.cos(wz), np.sin(wz)], axis=0)
    lane = np.arange(128)
    t, low = lane // 64, lane % 8
    wx = 2.0 * np.pi / 1024.0 * (k[:, None] * low[None, :])
    sign = np.where(t == 0, 1.0, -1.0)[None, :]
    twx = np.concatenate([np.cos(wx), np.sin(wx) * sign], axis=0)
    same = (lane // 8 % 8)[:, None] == (lane // 8 % 8)[None, :]
    w8 = 2.0 * np.pi / 8.0 * (low[:, None] * low[None, :] % 8)
    ta, tb = t[:, None], t[None, :]
    cos8, sin8 = np.cos(w8) * same, np.sin(w8) * same
    fwd = np.where(ta == tb, cos8, np.where(ta == 1, sin8, -sin8))
    inv = np.where(ta == tb, cos8, np.where(ta == 1, -sin8, sin8))
    fwd2 = np.concatenate([fwd, np.roll(fwd, 64, axis=0)], axis=0)
    inv2 = np.concatenate([inv, np.roll(inv, 64, axis=1)], axis=1)
    return [np.asarray(a, np.float32) for a in (dft, twz, twx, fwd2, inv2)]


def dot(a, b, ca=1, cb=0):
    return lax.dot_general(
        a, b, (((ca,), (cb,)), ((), ())), precision=HIGH, preferred_element_type=jnp.float32
    )


def fft8(u, sign):
    def add(a, b):
        return (a[0] + b[0], a[1] + b[1])

    def sub(a, b):
        return (a[0] - b[0], a[1] - b[1])

    def turn(a):
        return (-a[1], a[0]) if sign > 0 else (a[1], -a[0])

    def fft4(v):
        e, f = add(v[0], v[2]), sub(v[0], v[2])
        g, h = add(v[1], v[3]), turn(sub(v[1], v[3]))
        return [add(e, g), add(f, h), sub(e, g), sub(f, h)]

    even, odd = fft4(u[0::2]), fft4(u[1::2])
    o1, o3 = odd[1], odd[3]
    t1, t3 = turn(o1), turn(o3)
    odd = [
        odd[0],
        ((o1[0] + t1[0]) * ROOT, (o1[1] + t1[1]) * ROOT),
        turn(odd[2]),
        ((t3[0] - o3[0]) * ROOT, (t3[1] - o3[1]) * ROOT),
    ]
    return [add(even[k], odd[k]) for k in range(4)] + [sub(even[k], odd[k]) for k in range(4)]


def z_forward(load, twz):
    blocks = []
    for c in range(5):
        u = fft8([(load(j, 2 * c), load(j, 2 * c + 1)) for j in range(8)], -1)
        real, imag = [], []
        for r in range(8):
            re, im = u[r]
            if r:
                co, si = twz[r : r + 1, :], twz[8 + r : 9 + r, :]
                re, im = re * co + im * si, im * co - re * si
            real.append(re)
            imag.append(im)
        re, im = jnp.concatenate(real, axis=0), jnp.concatenate(imag, axis=0)
        left = jnp.concatenate([re, im], axis=0)
        right = jnp.concatenate([im, -re], axis=0)
        blocks.append(jnp.concatenate([left, right], axis=1))
    return blocks


def z_inverse(parts, twz):
    v = []
    for r in range(8):
        lo, hi = slice(8 * r, 8 * r + 8), slice(64 + 8 * r, 72 + 8 * r)
        re = parts[lo, :128] - parts[hi, 128:]
        im = parts[hi, :128] + parts[lo, 128:]
        if r:
            co, si = twz[r : r + 1, :], twz[8 + r : 9 + r, :]
            re, im = re * co - im * si, im * co + re * si
        v.append((re, im))
    return fft8(v, 1)


def green(spec, kz_base, half, couple):
    row = lax.broadcasted_iota(jnp.int32, (128, 128), 0)
    lane = lax.broadcasted_iota(jnp.int32, (128, 128), 1)
    kx = row + 128 * (lane % 8)
    kz = kz_base + lane // 8 % 8
    fx = jnp.where(kx < 512, kx, kx - 1024).astype(jnp.float32)
    fz = jnp.where(kz < 512, kz, kz - 1024).astype(jnp.float32)
    xx, zz, xz = fx * fx, fz * fz, fx * fz
    size = xx + zz
    inv = 1.0 / jnp.where(size == 0.0, 1.0, size)
    p, q, r = xx * inv, zz * inv, xz * inv
    r = jnp.where((kx == 512) != (kz == 512), 0.0, r)
    s0, s2, s4, s3, s5 = spec
    even = s0 * p + s2 * q
    load = couple * (even + 2.0 * (s4 * r))
    return (
        2.0 * half * (s0 * p + s4 * r) - load * p,
        2.0 * half * (s2 * q + s4 * r) - load * q,
        half * (r * (s0 + s2) + s4 * (p + q)) - couple * (r * even + 2.0 * (s4 * (p * q))),
        half * (s5 * r + s3 * q),
        half * (s5 * p + s3 * r),
    )


def middle(rows, kz_base, half, couple, dft, twx, fwd2, inv2):
    lane = lax.broadcasted_iota(jnp.int32, (128, 128), 1)
    sign = jnp.where(lane < 64, 1.0, -1.0)
    cx, sx = twx[:128, :], twx[128:, :]
    spec = []
    for x in rows:
        other = swap(x) * sign
        x1 = dot(dft, jnp.concatenate([x, other], axis=0))
        spec.append(dot(jnp.concatenate([x1 * cx, -(x1 * sx)], axis=1), fwd2))
    out = []
    for new in green(spec, kz_base, half, couple):
        both = dot(new, inv2)
        y, ry = both[:, :128], both[:, 128:]
        y2 = y * cx - ry * sx
        ry2 = ry * cx + y * sx
        out.append(dot(dft, jnp.concatenate([y2, -(ry2 * sign)], axis=0)))
    return out


def swap(x):
    return pltpu.roll(x, 64, axis=1)


def stress_terms(moduli, labels):
    lam = jnp.where(labels == 1, moduli[2], moduli[0])
    mu = jnp.where(labels == 1, moduli[3], moduli[1])
    stiff = moduli[4] * labels.astype(jnp.float32)
    return lam, mu, stiff


def orient(normals, s):
    steps = normals.astype(jnp.float32)
    rows = lax.broadcasted_iota(jnp.int32, (64, 4), 0) // BLK == lax.broadcasted_iota(jnp.int32, (64, 4), 1)
    cols = lax.broadcasted_iota(jnp.int32, (8, 128), 0) == lax.broadcasted_iota(jnp.int32, (8, 128), 1) // BLK
    wide = dot(dot(rows.astype(jnp.float32), steps), cols.astype(jnp.float32))
    cosine, sine = jnp.ones_like(wide), jnp.zeros_like(wide)
    for k in range(1, ANGLES):
        here = jnp.abs(wide - k) < 0.5
        cosine = jnp.where(here, math.cos(math.pi / ANGLES * k), cosine)
        sine = jnp.where(here, math.sin(math.pi / ANGLES * k), sine)
    return cosine * cosine, sine * sine, cosine * sine


def law(e, lam, mu2, stiff, angle):
    cc, ss, cs = angle
    trace = lam * (e[0] + e[1] + e[2])
    normal = stiff * (cc * e[0] + ss * e[2] + 2.0 * cs * e[4])
    dyad = (cc, None, ss, None, cs, None)
    out = []
    for k in range(6):
        value = mu2 * e[k]
        if k < 3:
            value = value + trace
        if dyad[k] is not None:
            value = value + normal * dyad[k]
        out.append(value)
    return out


def kernel(
    zs, xs,
    moduli, mean, strain, labels, normals, dft_ref, twz_ref, twx_ref, fwd_ref, inv_ref,
    strain_out, stress_out,
    s1, r1, s2, r2, s3, r3, s4, r4,
    send, recv, ready,
):
    j = lax.axis_index("gz")
    i = lax.axis_index("gx")
    total = zs * xs
    me = zs * i + j

    barrier = pltpu.get_barrier_semaphore()
    for k in range(1, zs):
        pl.semaphore_signal(barrier, inc=1, device_id={"gz": lax.rem(j + k, zs), "gx": i}, device_id_type=MESH)
    for k in range(1, xs):
        pl.semaphore_signal(barrier, inc=1, device_id={"gz": j, "gx": lax.rem(i + k, xs)}, device_id_type=MESH)

    m = [moduli[k] for k in range(5)]
    lame_ref = 0.5 * (m[0] + m[2])
    shear_ref = 0.5 * (m[1] + m[3])
    for s in range(2):
        angle = orient(normals[s], s)
        lam, mu, stiff = stress_terms(m, labels[s])
        e = [strain[c, s] for c in range(6)]
        pol = law(e, lam - lame_ref, 2.0 * (mu - shear_ref), stiff, angle)
        for slot, c in enumerate(COMPS):
            for g in range(8):
                s1[g, 2 * slot + s] = pol[c][8 * g : 8 * g + 8, :]

    pl.semaphore_wait(barrier, zs + xs - 2)
    for k in range(1, xs):
        pl.semaphore_signal(ready, inc=1, device_id={"gz": j, "gx": lax.rem(i + k, xs)}, device_id_type=MESH)

    def z_exchange(src, dst, n):
        for k in range(1, zs):
            to = lax.rem(j + k, zs)
            pltpu.make_async_remote_copy(
                src_ref=src.at[to], dst_ref=dst.at[j], send_sem=send.at[n], recv_sem=recv.at[n],
                device_id={"gz": to, "gx": i}, device_id_type=MESH,
            ).start()
        dst[j] = src[j]
        pltpu.make_async_copy(dst.at[pl.ds(0, zs - 1)], dst.at[pl.ds(0, zs - 1)], recv.at[n]).wait()

    def all_exchange(src, dst, n):
        mine = pl.multiple_of(me * 8, 8)

        def step(k, carry):
            to = lax.rem(me + k, total)
            there = pl.multiple_of(to * 8, 8)
            pltpu.make_async_remote_copy(
                src_ref=src.at[pl.ds(there, 8), :], dst_ref=dst.at[pl.ds(mine, 8), :],
                send_sem=send.at[n], recv_sem=recv.at[n],
                device_id={"gz": lax.rem(to, zs), "gx": to // zs}, device_id_type=MESH,
            ).start()
            return carry

        lax.fori_loop(1, total, step, 0)
        dst[pl.ds(mine, 8), :] = src[pl.ds(mine, 8), :]
        rest = dst.at[pl.ds(0, 8 * (total - 1)), :]
        pltpu.make_async_copy(rest, rest, recv.at[n]).wait()

    z_exchange(s1, r1, 0)
    dft = dft_ref[...]
    twz = twz_ref[...]
    for c, block in enumerate(z_forward(lambda a, b: r1[a, b], twz)):
        s2[pl.ds(c, 128, stride=8), :] = dot(dft, block, 1, 1)

    pl.semaphore_wait(ready, xs - 1)
    all_exchange(s2, r2, 1)
    scale = -1.0 / (1024.0 * 1024.0)
    half = scale * 0.5 / shear_ref
    couple = scale * (lame_ref + shear_ref) / (shear_ref * (lame_ref + 2.0 * shear_ref))
    rows = [r2[pl.ds(c, 128, stride=8), :] for c in range(5)]
    out = middle(rows, 8 * me, half, couple, dft, twx_ref[...], fwd_ref[...], inv_ref[...])
    for c in range(5):
        s3[pl.ds(c, 128, stride=8), :] = out[c]

    all_exchange(s3, r3, 2)
    for c in range(5):
        w = r3[pl.ds(c, 128, stride=8), :]
        tiles = z_inverse(dot(w.T, dft), twz)
        for g in range(8):
            s4[g, 2 * c] = tiles[g][0]
            s4[g, 2 * c + 1] = tiles[g][1]

    z_exchange(s4, r4, 3)
    for s in range(2):
        angle = orient(normals[s], s)
        lam, mu, stiff = stress_terms(m, labels[s])
        e = [None] * 6
        for slot, c in enumerate(COMPS):
            e[c] = jnp.concatenate([r4[g, 2 * slot + s] for g in range(8)], axis=0) + mean[c]
        e[1] = jnp.full((64, 128), mean[1], jnp.float32)
        stress = law(e, lam, 2.0 * mu, stiff, angle)
        for c in range(6):
            strain_out[c, s] = e[c]
            stress_out[c, s] = stress[c]

    for n, ref in ((0, s1), (3, s4)):
        part = ref.at[pl.ds(0, zs - 1)]
        pltpu.make_async_copy(part, part, send.at[n]).wait()
    for n, ref in ((1, s2), (2, s3)):
        part = ref.at[pl.ds(0, 8 * (total - 1)), :]
        pltpu.make_async_copy(part, part, send.at[n]).wait()


def solution(mesh):
    zs, xs = mesh.shape["gz"], mesh.shape["gx"]
    consts = tables()

    def shards(strain, labels, normals, moduli, mean_strain):
        vmem = pl.BlockSpec(memory_space=pltpu.VMEM)
        smem = pl.BlockSpec(memory_space=pltpu.SMEM)
        tile = pltpu.VMEM((8, 10, 8, 128), jnp.float32)
        wide = pltpu.VMEM((1024, 128), jnp.float32)
        return tuple(
            pl.pallas_call(
                functools.partial(kernel, zs, xs),
                out_shape=[jax.ShapeDtypeStruct(strain.shape, jnp.float32)] * 2,
                in_specs=[smem, smem] + [vmem] * 8,
                out_specs=[vmem, vmem],
                scratch_shapes=[tile, tile, wide, wide, wide, wide, tile, tile]
                + [pltpu.SemaphoreType.DMA((4,)), pltpu.SemaphoreType.DMA((4,)), pltpu.SemaphoreType.REGULAR],
                compiler_params=pltpu.CompilerParams(collective_id=0, has_side_effects=True),
            )(moduli, mean_strain, strain, labels, normals, *[jnp.asarray(a) for a in consts])
        )

    in_specs = (P(None, None, "gx", "gz"), P(None, "gx", "gz"), P(None, "gx", "gz"), P(), P())
    out_specs = (P(None, None, "gx", "gz"), P(None, None, "gx", "gz"))
    return jax.shard_map(shards, mesh=mesh, in_specs=in_specs, out_specs=out_specs, check_vma=False)
```

profile of v0, /device:TPU:1, one launch (start us, length us, event | category | flops | bytes accessed | tf_op | source)
XLA Modules:
  0.0 51.9 jit_solution(5458575601345423912)
XLA Ops:
  0.6 48.7 %shard_map.113 = (f32[6,2,64,128]{3,2,1,0:T(8,128)}, f32[6,2,64,128]{3,2,1,0:T(8,128)}) custom-call(f32[5]{0:T(128)} %moduli.1, f32[6]{0:T(128)} %mean.1, f32[6,2,64,128]{3,2,1,0:T(8,128)} %strain.1, s32[2,64,128]{2,1,0:T(8,128)} %labels.1, s32[2,4,8]{2,1,0:T(4,128)} %normals.1, f32[128,256]{1,0:T(8,128)} %constant.10.clone.dft_ref, ...), custom_call_target="tpu_custom_call" | custom-call | tf_op jit(solution)/shard_map/pallas_call | solution.py:308
  49.3 0.0 copy-start
  49.3 1.8 %copy.14 = f32[6,2,64,128]{3,2,1,0:T(8,128)} copy(f32[6,2,64,128]{3,2,1,0:T(8,128)} %get-tuple-element.4) | data formatting | bytes 786432
  51.1 0.0 copy-done
  51.1 0.7 %copy.15 = f32[6,2,64,128]{3,2,1,0:T(8,128)} copy(f32[6,2,64,128]{3,2,1,0:T(8,128)S(1)} %copy-done) | data formatting | bytes 786432
Async XLA Ops:
  49.3 1.8 %copy-start = (f32[6,2,64,128]{3,2,1,0:T(8,128)S(1)}, f32[6,2,64,128]{3,2,1,0:T(8,128)}, u32[]{:S(2)}) copy-start(f32[6,2,64,128]{3,2,1,0:T(8,128)} %get-tuple-element.5) | copy-start | bytes 1179652
where the time goes:
time: 52 us; the launch traced here: 51.9 us
  Pallas kernels  48.7 us (94%)
  local copies, waits for them, and re-layouts  2.57 us (5%)
  between operations  0.65 us (1%)
    pallas_call x1, Pallas kernels, shards(): pl.pallas_call(functools.partial(kernel, zs, xs), out_shape=[jax.ShapeDty...  48.7 us
    unnamed x4, local copies, waits for them, and re-layouts  2.57 us

commit v1 on v0

--- a/solution.py
+++ b/solution.py
@@ -1,4 +1,4 @@
-import functools
+import itertools
 import math
 
 import jax
@@ -37,12 +37,39 @@
     inv = np.where(ta == tb, cos8, np.where(ta == 1, -sin8, sin8))
     fwd2 = np.concatenate([fwd, np.roll(fwd, 64, axis=0)], axis=0)
     inv2 = np.concatenate([inv, np.roll(inv, 64, axis=1)], axis=1)
-    return [np.asarray(a, np.float32) for a in (dft, twz, twx, fwd2, inv2)]
-
-
-def dot(a, b, ca=1, cb=0):
+    twz, twx = np.asarray(twz, np.float32), np.asarray(twx, np.float32)
+    return [left_table(dft), right_table(dft), right_table(fwd2), right_table(inv2), twz, twx]
+
+
+def halves(a):
+    a = np.asarray(a, np.float32)
+    high = a.astype(jnp.bfloat16)
+    return high, (a - high.astype(np.float32)).astype(jnp.bfloat16)
+
+
+def left_table(a):
+    high, low = halves(a)
+    return np.concatenate([high, low, high], axis=1)
+
+
+def right_table(a):
+    high, low = halves(a)
+    return np.concatenate([high, low, high], axis=0)
+
+
+def split3(x, axis):
+    high = x.astype(jnp.bfloat16)
+    low = (x - high.astype(jnp.float32)).astype(jnp.bfloat16)
+    return jnp.concatenate([high, high, low], axis=axis)
+
+
+def mul(a, b, ca=1, cb=0):
+    return lax.dot_general(a, b, (((ca,), (cb,)), ((), ())), preferred_element_type=jnp.float32)
+
+
+def dot(a, b):
     return lax.dot_general(
-        a, b, (((ca,), (cb,)), ((), ())), precision=HIGH, preferred_element_type=jnp.float32
+        a, b, (((1,), (0,)), ((), ())), precision=HIGH, preferred_element_type=jnp.float32
     )
 
 
@@ -89,7 +116,7 @@
         left = jnp.concatenate([re, im], axis=0)
         right = jnp.concatenate([im, -re], axis=0)
         blocks.append(jnp.concatenate([left, right], axis=1))
-    return blocks
+    return jnp.concatenate(blocks, axis=0)
 
 
 def z_inverse(parts, twz):
@@ -129,23 +156,30 @@
     )
 
 
-def middle(rows, kz_base, half, couple, dft, twx, fwd2, inv2):
+def middle(wide, kz_base, half, couple, tabs):
+    left, _, fwd, inv, _, twx = tabs
+    n = len(COMPS)
     lane = lax.broadcasted_iota(jnp.int32, (128, 128), 1)
     sign = jnp.where(lane < 64, 1.0, -1.0)
     cx, sx = twx[:128, :], twx[128:, :]
-    spec = []
-    for x in rows:
-        other = swap(x) * sign
-        x1 = dot(dft, jnp.concatenate([x, other], axis=0))
-        spec.append(dot(jnp.concatenate([x1 * cx, -(x1 * sx)], axis=1), fwd2))
+
+    def lanes(x, c):
+        return x[:, 128 * c : 128 * c + 128]
+
+    def rows(x, c):
+        return x[128 * c : 128 * c + 128]
+
+    pairs = [jnp.concatenate([lanes(wide, c), swap(lanes(wide, c)) * sign], axis=0) for c in range(n)]
+    x1 = mul(left, split3(jnp.concatenate(pairs, axis=1), 0))
+    turned = [jnp.concatenate([lanes(x1, c) * cx, -(lanes(x1, c) * sx)], axis=1) for c in range(n)]
+    spec = mul(split3(jnp.concatenate(turned, axis=0), 1), fwd)
+    new = green([rows(spec, c) for c in range(n)], kz_base, half, couple)
+    both = mul(split3(jnp.concatenate(new, axis=0), 1), inv)
     out = []
-    for new in green(spec, kz_base, half, couple):
-        both = dot(new, inv2)
-        y, ry = both[:, :128], both[:, 128:]
-        y2 = y * cx - ry * sx
-        ry2 = ry * cx + y * sx
-        out.append(dot(dft, jnp.concatenate([y2, -(ry2 * sign)], axis=0)))
-    return out
+    for c in range(n):
+        y, ry = rows(both, c)[:, :128], rows(both, c)[:, 128:]
+        out.append(jnp.concatenate([y * cx - ry * sx, -((ry * cx + y * sx) * sign)], axis=0))
+    return mul(left, split3(jnp.concatenate(out, axis=1), 0))
 
 
 def swap(x):
@@ -188,23 +222,60 @@
     return out
 
 
+def far_first(sizes, hops):
+    offsets = [o for o in itertools.product(*[range(n) for n in sizes]) if any(o)]
+    return sorted(offsets, key=lambda o: -sum(h(v) for h, v in zip(hops, o)))
+
+
+def ring(v):
+    return min(v, 4 - v)
+
+
 def kernel(
-    zs, xs,
-    moduli, mean, strain, labels, normals, dft_ref, twz_ref, twx_ref, fwd_ref, inv_ref,
+    moduli, mean, strain_hbm, labels_hbm, normals_hbm, left_hbm, right_hbm, fwd_hbm, inv_hbm, twz_hbm, twx_hbm,
     strain_out, stress_out,
+    strain, labels, normals, left_ref, right_ref, fwd_ref, inv_ref, twz_ref, twx_ref,
     s1, r1, s2, r2, s3, r3, s4, r4,
-    send, recv, ready,
+    load, send, recv, ready,
 ):
+    zs, xs = lax.axis_size("gz"), lax.axis_size("gx")
+    total = zs * xs
     j = lax.axis_index("gz")
     i = lax.axis_index("gx")
-    total = zs * xs
     me = zs * i + j
+    z, x, core = j // 2, i // 4, lax.rem(i, 2)
+    y = 2 * lax.rem(j, 2) + lax.rem(i // 2, 2)
+
+    def peer(dx, dy, dz, dc):
+        px, py, pz, pc = lax.rem(x + dx, 4), lax.rem(y + dy, 4), lax.rem(z + dz, 4), lax.rem(core + dc, 2)
+        return 2 * pz + py // 2, 4 * px + 2 * lax.rem(py, 2) + pc
+
+    z_peers = [peer(0, dy, dz, 0) for dz, dy in far_first((4, 3), (ring, ring)) if dy != 1]
+    everyone = far_first((4, 4, 4, 2), (ring, ring, ring, lambda v: 0))
+
+    def x_index(dx, dy, dc):
+        low = lax.rem(i // 2 + dy, 2)
+        return 4 * lax.rem(x + dx, 4) + 2 * low + lax.rem(core + dc, 2)
+
+    x_peers = [x_index(*o) for o in far_first((4, 2, 2), (ring, lambda v: v, lambda v: 0))]
 
     barrier = pltpu.get_barrier_semaphore()
-    for k in range(1, zs):
-        pl.semaphore_signal(barrier, inc=1, device_id={"gz": lax.rem(j + k, zs), "gx": i}, device_id_type=MESH)
-    for k in range(1, xs):
-        pl.semaphore_signal(barrier, inc=1, device_id={"gz": j, "gx": lax.rem(i + k, xs)}, device_id_type=MESH)
+    for to, _ in z_peers:
+        pl.semaphore_signal(barrier, inc=1, device_id={"gz": to, "gx": i}, device_id_type=MESH)
+    for to in x_peers:
+        pl.semaphore_signal(barrier, inc=1, device_id={"gz": j, "gx": to}, device_id_type=MESH)
+
+    loads = [
+        pltpu.make_async_copy(a, b, load.at[k])
+        for k, (a, b) in enumerate((
+            (strain_hbm, strain), (labels_hbm, labels), (normals_hbm, normals), (twz_hbm, twz_ref),
+            (left_hbm, left_ref), (twx_hbm, twx_ref), (fwd_hbm, fwd_ref), (inv_hbm, inv_ref), (right_hbm, right_ref),
+        ))
+    ]
+    for copy in loads:
+        copy.start()
+    for copy in loads[:3]:
+        copy.wait()
 
     m = [moduli[k] for k in range(5)]
     lame_ref = 0.5 * (m[0] + m[2])
@@ -219,12 +290,11 @@
                 s1[g, 2 * slot + s] = pol[c][8 * g : 8 * g + 8, :]
 
     pl.semaphore_wait(barrier, zs + xs - 2)
-    for k in range(1, xs):
-        pl.semaphore_signal(ready, inc=1, device_id={"gz": j, "gx": lax.rem(i + k, xs)}, device_id_type=MESH)
+    for to in x_peers:
+        pl.semaphore_signal(ready, inc=1, device_id={"gz": j, "gx": to}, device_id_type=MESH)
 
     def z_exchange(src, dst, n):
-        for k in range(1, zs):
-            to = lax.rem(j + k, zs)
+        for to, _ in z_peers:
             pltpu.make_async_remote_copy(
                 src_ref=src.at[to], dst_ref=dst.at[j], send_sem=send.at[n], recv_sem=recv.at[n],
                 device_id={"gz": to, "gx": i}, device_id_type=MESH,
@@ -234,42 +304,44 @@
 
     def all_exchange(src, dst, n):
         mine = pl.multiple_of(me * 8, 8)
-
-        def step(k, carry):
-            to = lax.rem(me + k, total)
-            there = pl.multiple_of(to * 8, 8)
+        for o in everyone:
+            tz, tx = peer(*o)
+            there = pl.multiple_of((zs * tx + tz) * 8, 8)
             pltpu.make_async_remote_copy(
-                src_ref=src.at[pl.ds(there, 8), :], dst_ref=dst.at[pl.ds(mine, 8), :],
+                src_ref=src.at[pl.ds(there, 5), :], dst_ref=dst.at[pl.ds(mine, 5), :],
                 send_sem=send.at[n], recv_sem=recv.at[n],
-                device_id={"gz": lax.rem(to, zs), "gx": to // zs}, device_id_type=MESH,
+                device_id={"gz": tz, "gx": tx}, device_id_type=MESH,
             ).start()
-            return carry
-
-        lax.fori_loop(1, total, step, 0)
         dst[pl.ds(mine, 8), :] = src[pl.ds(mine, 8), :]
-        rest = dst.at[pl.ds(0, 8 * (total - 1)), :]
+        rest = dst.at[pl.ds(0, 5 * (total - 1)), :]
         pltpu.make_async_copy(rest, rest, recv.at[n]).wait()
 
+    def gathered(ref):
+        return [ref[pl.ds(c, 128, stride=8), :] for c in range(5)]
+
+    def scatter(ref, value):
+        for c in range(5):
+            ref[pl.ds(c, 128, stride=8), :] = value[:, 128 * c : 128 * c + 128]
+
     z_exchange(s1, r1, 0)
-    dft = dft_ref[...]
-    twz = twz_ref[...]
-    for c, block in enumerate(z_forward(lambda a, b: r1[a, b], twz)):
-        s2[pl.ds(c, 128, stride=8), :] = dot(dft, block, 1, 1)
+    for copy in loads[3:]:
+        copy.wait()
+    tabs = [ref[...] for ref in (left_ref, right_ref, fwd_ref, inv_ref, twz_ref, twx_ref)]
+    twz = tabs[4]
+    scatter(s2, mul(tabs[0], split3(z_forward(lambda a, b: r1[a, b], twz), 1), 1, 1))
 
     pl.semaphore_wait(ready, xs - 1)
     all_exchange(s2, r2, 1)
     scale = -1.0 / (1024.0 * 1024.0)
     half = scale * 0.5 / shear_ref
     couple = scale * (lame_ref + shear_ref) / (shear_ref * (lame_ref + 2.0 * shear_ref))
-    rows = [r2[pl.ds(c, 128, stride=8), :] for c in range(5)]
-    out = middle(rows, 8 * me, half, couple, dft, twx_ref[...], fwd_ref[...], inv_ref[...])
+    scatter(s3, middle(jnp.concatenate(gathered(r2), axis=1), 8 * me, half, couple, tabs))
+
+    all_exchange(s3, r3, 2)
+    flat = jnp.concatenate([w.T for w in gathered(r3)], axis=0)
+    parts = mul(split3(flat, 1), tabs[1])
     for c in range(5):
-        s3[pl.ds(c, 128, stride=8), :] = out[c]
-
-    all_exchange(s3, r3, 2)
-    for c in range(5):
-        w = r3[pl.ds(c, 128, stride=8), :]
-        tiles = z_inverse(dot(w.T, dft), twz)
+        tiles = z_inverse(parts[128 * c : 128 * c + 128], twz)
         for g in range(8):
             s4[g, 2 * c] = tiles[g][0]
             s4[g, 2 * c + 1] = tiles[g][1]
@@ -291,29 +363,32 @@
         part = ref.at[pl.ds(0, zs - 1)]
         pltpu.make_async_copy(part, part, send.at[n]).wait()
     for n, ref in ((1, s2), (2, s3)):
-        part = ref.at[pl.ds(0, 8 * (total - 1)), :]
+        part = ref.at[pl.ds(0, 5 * (total - 1)), :]
         pltpu.make_async_copy(part, part, send.at[n]).wait()
 
 
 def solution(mesh):
-    zs, xs = mesh.shape["gz"], mesh.shape["gx"]
     consts = tables()
 
     def shards(strain, labels, normals, moduli, mean_strain):
         vmem = pl.BlockSpec(memory_space=pltpu.VMEM)
         smem = pl.BlockSpec(memory_space=pltpu.SMEM)
+        away = pl.BlockSpec(memory_space=pl.ANY)
+        arrays = [strain, labels, normals] + [jnp.asarray(a) for a in consts]
         tile = pltpu.VMEM((8, 10, 8, 128), jnp.float32)
         wide = pltpu.VMEM((1024, 128), jnp.float32)
         return tuple(
             pl.pallas_call(
-                functools.partial(kernel, zs, xs),
-                out_shape=[jax.ShapeDtypeStruct(strain.shape, jnp.float32)] * 2,
-                in_specs=[smem, smem] + [vmem] * 8,
+                kernel,
+                out_shape=[pltpu.VMEM(strain.shape, jnp.float32)] * 2,
+                in_specs=[smem, smem] + [away] * len(arrays),
                 out_specs=[vmem, vmem],
-                scratch_shapes=[tile, tile, wide, wide, wide, wide, tile, tile]
-                + [pltpu.SemaphoreType.DMA((4,)), pltpu.SemaphoreType.DMA((4,)), pltpu.SemaphoreType.REGULAR],
+                scratch_shapes=[pltpu.VMEM(a.shape, a.dtype) for a in arrays]
+                + [tile, tile, wide, wide, wide, wide, tile, tile]
+                + [pltpu.SemaphoreType.DMA((len(arrays),)), pltpu.SemaphoreType.DMA((4,))]
+                + [pltpu.SemaphoreType.DMA((4,)), pltpu.SemaphoreType.REGULAR],
                 compiler_params=pltpu.CompilerParams(collective_id=0, has_side_effects=True),
-            )(moduli, mean_strain, strain, labels, normals, *[jnp.asarray(a) for a in consts])
+            )(moduli, mean_strain, *arrays)
         )
 
     in_specs = (P(None, None, "gx", "gz"), P(None, "gx", "gz"), P(None, "gx", "gz"), P(), P())

time: 52 us -> 40.8 us (0.78)
  Pallas kernels: 48.7 us -> 38.5 us
  local copies, waits for them, and re-layouts: 2.57 us -> 1.49 us
    pallas_call x1, Pallas kernels: 48.7 us -> 38.5 us  [shards(): pl.pallas_call(kernel, out_shape=[pltpu.VMEM(strain.shape, jnp.float32)]...]
    unnamed x4 -> x2, local copies, waits for them, and re-layouts: 2.57 us -> 1.49 us
where the time goes in v1:
time: 40.8 us; the launch traced here: 40.6 us
  Pallas kernels  38.5 us (94%)
  local copies, waits for them, and re-layouts  1.49 us (4%)
  between operations  0.64 us (2%)
    pallas_call x1, Pallas kernels, shards(): pl.pallas_call(kernel, out_shape=[pltpu.VMEM(strain.shape, jnp.float32)]...  38.5 us
    unnamed x2, local copies, waits for them, and re-layouts  1.49 us

profile of v1, /device:TPU:1, one launch (start us, length us, event | category | flops | bytes accessed | tf_op | source)
XLA Modules:
  0.0 40.6 jit_solution(929926632145642690)
XLA Ops:
  0.6 38.5 %shard_map.122 = (f32[6,2,64,128]{3,2,1,0:T(8,128)S(1)}, f32[6,2,64,128]{3,2,1,0:T(8,128)S(1)}) custom-call(f32[5]{0:T(128)} %moduli.1, f32[6]{0:T(128)} %mean.1, f32[6,2,64,128]{3,2,1,0:T(8,128)} %strain_hbm.1, s32[2,64,128]{2,1,0:T(8,128)} %labels_hbm.1, s32[2,4,8]{2,1,0:T(4,128)} %normals_hbm.1, bf16[128,768]{1,0:T(8,128)(2,1)} %constant.12.clone.left_hbm, ...), custom_call_target="tpu_custom_call" | custom-call | tf_op jit(solution)/shard_map/pallas_call | solution.py:381
  39.1 0.7 %copy.15 = f32[6,2,64,128]{3,2,1,0:T(8,128)} copy(f32[6,2,64,128]{3,2,1,0:T(8,128)S(1)} %get-tuple-element.2) | data formatting | bytes 786432
  39.9 0.7 %copy.16 = f32[6,2,64,128]{3,2,1,0:T(8,128)} copy(f32[6,2,64,128]{3,2,1,0:T(8,128)S(1)} %get-tuple-element.3) | data formatting | bytes 786432

commit v2 on v1

--- a/solution.py
+++ b/solution.py
@@ -12,6 +12,7 @@
 ANGLES = 8
 BLK = 16
 COMPS = (0, 2, 4, 3, 5)
+GROUPS = ((0, 3), (3, 2))
 MESH = pl.DeviceIdType.MESH
 HIGH = lax.Precision.HIGHEST
 ROOT = math.sqrt(0.5)
@@ -100,9 +101,9 @@
     return [add(even[k], odd[k]) for k in range(4)] + [sub(even[k], odd[k]) for k in range(4)]
 
 
-def z_forward(load, twz):
+def z_forward(load, twz, slots):
     blocks = []
-    for c in range(5):
+    for c in slots:
         u = fft8([(load(j, 2 * c), load(j, 2 * c + 1)) for j in range(8)], -1)
         real, imag = [], []
         for r in range(8):
@@ -132,7 +133,7 @@
     return fft8(v, 1)
 
 
-def green(spec, kz_base, half, couple):
+def green_maps(kz_base):
     row = lax.broadcasted_iota(jnp.int32, (128, 128), 0)
     lane = lax.broadcasted_iota(jnp.int32, (128, 128), 1)
     kx = row + 128 * (lane % 8)
@@ -143,22 +144,27 @@
     size = xx + zz
     inv = 1.0 / jnp.where(size == 0.0, 1.0, size)
     p, q, r = xx * inv, zz * inv, xz * inv
-    r = jnp.where((kx == 512) != (kz == 512), 0.0, r)
-    s0, s2, s4, s3, s5 = spec
-    even = s0 * p + s2 * q
-    load = couple * (even + 2.0 * (s4 * r))
+    return p, q, jnp.where((kx == 512) != (kz == 512), 0.0, r), p * q
+
+
+def green(spec, maps, half, couple):
+    p, q, r, pq = maps
+    if len(spec) == 2:
+        s3, s5 = spec
+        return half * (s5 * r + s3 * q), half * (s5 * p + s3 * r)
+    s0, s2, s4 = spec
+    even, cross = s0 * p + s2 * q, s4 * r
+    load = couple * (even + 2.0 * cross)
     return (
-        2.0 * half * (s0 * p + s4 * r) - load * p,
-        2.0 * half * (s2 * q + s4 * r) - load * q,
-        half * (r * (s0 + s2) + s4 * (p + q)) - couple * (r * even + 2.0 * (s4 * (p * q))),
-        half * (s5 * r + s3 * q),
-        half * (s5 * p + s3 * r),
+        2.0 * half * (s0 * p + cross) - load * p,
+        2.0 * half * (s2 * q + cross) - load * q,
+        half * (r * (s0 + s2) + s4 * (p + q)) - couple * (r * even + 2.0 * (s4 * pq)),
     )
 
 
-def middle(wide, kz_base, half, couple, tabs):
+def middle(wide, maps, half, couple, tabs):
     left, _, fwd, inv, _, twx = tabs
-    n = len(COMPS)
+    n = wide.shape[1] // 128
     lane = lax.broadcasted_iota(jnp.int32, (128, 128), 1)
     sign = jnp.where(lane < 64, 1.0, -1.0)
     cx, sx = twx[:128, :], twx[128:, :]
@@ -173,7 +179,7 @@
     x1 = mul(left, split3(jnp.concatenate(pairs, axis=1), 0))
     turned = [jnp.concatenate([lanes(x1, c) * cx, -(lanes(x1, c) * sx)], axis=1) for c in range(n)]
     spec = mul(split3(jnp.concatenate(turned, axis=0), 1), fwd)
-    new = green([rows(spec, c) for c in range(n)], kz_base, half, couple)
+    new = green([rows(spec, c) for c in range(n)], maps, half, couple)
     both = mul(split3(jnp.concatenate(new, axis=0), 1), inv)
     out = []
     for c in range(n):
@@ -235,7 +241,7 @@
     moduli, mean, strain_hbm, labels_hbm, normals_hbm, left_hbm, right_hbm, fwd_hbm, inv_hbm, twz_hbm, twx_hbm,
     strain_out, stress_out,
     strain, labels, normals, left_ref, right_ref, fwd_ref, inv_ref, twz_ref, twx_ref,
-    s1, r1, s2, r2, s3, r3, s4, r4,
+    s1, r1, s2, r2, s3, r3, s4, r4, cells, maps,
     load, send, recv, ready,
 ):
     zs, xs = lax.axis_size("gz"), lax.axis_size("gx")
@@ -246,9 +252,14 @@
     z, x, core = j // 2, i // 4, lax.rem(i, 2)
     y = 2 * lax.rem(j, 2) + lax.rem(i // 2, 2)
 
+    px = [4 * lax.rem(x + d, 4) for d in range(4)]
+    py = [lax.rem(y + d, 4) for d in range(4)]
+    pz = [2 * lax.rem(z + d, 4) for d in range(4)]
+    pc = [lax.rem(core + d, 2) for d in range(2)]
+    high, low = [v // 2 for v in py], [2 * lax.rem(v, 2) for v in py]
+
     def peer(dx, dy, dz, dc):
-        px, py, pz, pc = lax.rem(x + dx, 4), lax.rem(y + dy, 4), lax.rem(z + dz, 4), lax.rem(core + dc, 2)
-        return 2 * pz + py // 2, 4 * px + 2 * lax.rem(py, 2) + pc
+        return pz[dz] + high[dy], px[dx] + low[dy] + pc[dc]
 
     z_peers = [peer(0, dy, dz, 0) for dz, dy in far_first((4, 3), (ring, ring)) if dy != 1]
     everyone = far_first((4, 4, 4, 2), (ring, ring, ring, lambda v: 0))
@@ -288,83 +299,112 @@
         for slot, c in enumerate(COMPS):
             for g in range(8):
                 s1[g, 2 * slot + s] = pol[c][8 * g : 8 * g + 8, :]
+        for k, value in enumerate((lam, 2.0 * mu, stiff, *angle)):
+            cells[s, k] = value
 
     pl.semaphore_wait(barrier, zs + xs - 2)
     for to in x_peers:
         pl.semaphore_signal(ready, inc=1, device_id={"gz": j, "gx": to}, device_id_type=MESH)
 
-    def z_exchange(src, dst, n):
+    def z_send(src, dst, n, g):
+        part = pl.ds(2 * GROUPS[g][0], 2 * GROUPS[g][1])
         for to, _ in z_peers:
             pltpu.make_async_remote_copy(
-                src_ref=src.at[to], dst_ref=dst.at[j], send_sem=send.at[n], recv_sem=recv.at[n],
+                src_ref=src.at[to, part], dst_ref=dst.at[j, part], send_sem=send.at[n, g], recv_sem=recv.at[n, g],
                 device_id={"gz": to, "gx": i}, device_id_type=MESH,
             ).start()
-        dst[j] = src[j]
-        pltpu.make_async_copy(dst.at[pl.ds(0, zs - 1)], dst.at[pl.ds(0, zs - 1)], recv.at[n]).wait()
-
-    def all_exchange(src, dst, n):
+        dst[j, part] = src[j, part]
+
+    def z_wait(ref, sem, n, g):
+        part = ref.at[pl.ds(0, zs - 1), pl.ds(2 * GROUPS[g][0], 2 * GROUPS[g][1])]
+        pltpu.make_async_copy(part, part, sem.at[n, g]).wait()
+
+    def all_send(src, dst, n, g):
         mine = pl.multiple_of(me * 8, 8)
+        size = GROUPS[g][1]
         for o in everyone:
             tz, tx = peer(*o)
             there = pl.multiple_of((zs * tx + tz) * 8, 8)
             pltpu.make_async_remote_copy(
-                src_ref=src.at[pl.ds(there, 5), :], dst_ref=dst.at[pl.ds(mine, 5), :],
-                send_sem=send.at[n], recv_sem=recv.at[n],
+                src_ref=src.at[g, pl.ds(there, size), :], dst_ref=dst.at[g, pl.ds(mine, size), :],
+                send_sem=send.at[n, g], recv_sem=recv.at[n, g],
                 device_id={"gz": tz, "gx": tx}, device_id_type=MESH,
             ).start()
-        dst[pl.ds(mine, 8), :] = src[pl.ds(mine, 8), :]
-        rest = dst.at[pl.ds(0, 5 * (total - 1)), :]
-        pltpu.make_async_copy(rest, rest, recv.at[n]).wait()
-
-    def gathered(ref):
-        return [ref[pl.ds(c, 128, stride=8), :] for c in range(5)]
-
-    def scatter(ref, value):
-        for c in range(5):
-            ref[pl.ds(c, 128, stride=8), :] = value[:, 128 * c : 128 * c + 128]
-
-    z_exchange(s1, r1, 0)
-    for copy in loads[3:]:
-        copy.wait()
-    tabs = [ref[...] for ref in (left_ref, right_ref, fwd_ref, inv_ref, twz_ref, twx_ref)]
-    twz = tabs[4]
-    scatter(s2, mul(tabs[0], split3(z_forward(lambda a, b: r1[a, b], twz), 1), 1, 1))
-
-    pl.semaphore_wait(ready, xs - 1)
-    all_exchange(s2, r2, 1)
+        dst[g, pl.ds(mine, 8), :] = src[g, pl.ds(mine, 8), :]
+
+    def all_wait(ref, sem, n, g):
+        part = ref.at[g, pl.ds(0, GROUPS[g][1] * (total - 1)), :]
+        pltpu.make_async_copy(part, part, sem.at[n, g]).wait()
+
+    def gathered(ref, g):
+        return [ref[g, pl.ds(c, 128, stride=8), :] for c in range(GROUPS[g][1])]
+
+    def scatter(ref, g, value):
+        for c in range(GROUPS[g][1]):
+            ref[g, pl.ds(c, 128, stride=8), :] = value[:, 128 * c : 128 * c + 128]
+
+    for g in range(2):
+        z_send(s1, r1, 0, g)
     scale = -1.0 / (1024.0 * 1024.0)
     half = scale * 0.5 / shear_ref
     couple = scale * (lame_ref + shear_ref) / (shear_ref * (lame_ref + 2.0 * shear_ref))
-    scatter(s3, middle(jnp.concatenate(gathered(r2), axis=1), 8 * me, half, couple, tabs))
-
-    all_exchange(s3, r3, 2)
-    flat = jnp.concatenate([w.T for w in gathered(r3)], axis=0)
-    parts = mul(split3(flat, 1), tabs[1])
-    for c in range(5):
-        tiles = z_inverse(parts[128 * c : 128 * c + 128], twz)
-        for g in range(8):
-            s4[g, 2 * c] = tiles[g][0]
-            s4[g, 2 * c + 1] = tiles[g][1]
-
-    z_exchange(s4, r4, 3)
-    for s in range(2):
-        angle = orient(normals[s], s)
-        lam, mu, stiff = stress_terms(m, labels[s])
-        e = [None] * 6
-        for slot, c in enumerate(COMPS):
-            e[c] = jnp.concatenate([r4[g, 2 * slot + s] for g in range(8)], axis=0) + mean[c]
-        e[1] = jnp.full((64, 128), mean[1], jnp.float32)
-        stress = law(e, lam, 2.0 * mu, stiff, angle)
-        for c in range(6):
-            strain_out[c, s] = e[c]
-            stress_out[c, s] = stress[c]
-
-    for n, ref in ((0, s1), (3, s4)):
-        part = ref.at[pl.ds(0, zs - 1)]
-        pltpu.make_async_copy(part, part, send.at[n]).wait()
-    for n, ref in ((1, s2), (2, s3)):
-        part = ref.at[pl.ds(0, 5 * (total - 1)), :]
-        pltpu.make_async_copy(part, part, send.at[n]).wait()
+    for k, value in enumerate(green_maps(8 * me)):
+        maps[k] = value
+    for copy in loads[3:]:
+        copy.wait()
+
+    def table(ref):
+        return ref[...]
+
+    for g, (first, size) in enumerate(GROUPS):
+        z_wait(r1, recv, 0, g)
+        block = z_forward(lambda a, b: r1[a, b], table(twz_ref), range(first, first + size))
+        scatter(s2, g, mul(table(left_ref), split3(block, 1), 1, 1))
+        if g == 0:
+            pl.semaphore_wait(ready, xs - 1)
+        all_send(s2, r2, 1, g)
+
+    for g in range(2):
+        all_wait(r2, recv, 1, g)
+        tabs = [table(ref) for ref in (left_ref, right_ref, fwd_ref, inv_ref, twz_ref, twx_ref)]
+        wide = jnp.concatenate(gathered(r2, g), axis=1)
+        scatter(s3, g, middle(wide, [maps[k] for k in range(4)], half, couple, tabs))
+        all_send(s3, r3, 2, g)
+
+    for g, (first, size) in enumerate(GROUPS):
+        all_wait(r3, recv, 2, g)
+        flat = jnp.concatenate([w.T for w in gathered(r3, g)], axis=0)
+        parts = mul(split3(flat, 1), table(right_ref))
+        for c in range(size):
+            tiles = z_inverse(parts[128 * c : 128 * c + 128], table(twz_ref))
+            for k in range(8):
+                s4[k, 2 * (first + c)] = tiles[k][0]
+                s4[k, 2 * (first + c) + 1] = tiles[k][1]
+        z_send(s4, r4, 3, g)
+
+    for g in range(2):
+        z_wait(s1, send, 0, g)
+        all_wait(s2, send, 1, g)
+        all_wait(s3, send, 2, g)
+
+    def arrived(slot, s):
+        return jnp.concatenate([r4[k, 2 * slot + s] for k in range(8)], axis=0) + mean[COMPS[slot]]
+
+    for g, (first, size) in enumerate(GROUPS):
+        z_wait(r4, recv, 3, g)
+        for s in range(2):
+            e = [jnp.full((64, 128), mean[1], jnp.float32)] * 6
+            for slot in range(first, first + size):
+                e[COMPS[slot]] = arrived(slot, s)
+            lam, mu2, stiff = (cells[s, k] for k in range(3))
+            stress = law(e, lam, mu2, stiff, [cells[s, k] for k in range(3, 6)])
+            done = [COMPS[k] for k in range(first, first + size)] + [1] * (g == 0)
+            for c in done:
+                strain_out[c, s] = e[c]
+                stress_out[c, s] = stress[c]
+
+    for g in range(2):
+        z_wait(s4, send, 3, g)
 
 
 def solution(mesh):
@@ -376,7 +416,7 @@
         away = pl.BlockSpec(memory_space=pl.ANY)
         arrays = [strain, labels, normals] + [jnp.asarray(a) for a in consts]
         tile = pltpu.VMEM((8, 10, 8, 128), jnp.float32)
-        wide = pltpu.VMEM((1024, 128), jnp.float32)
+        wide = pltpu.VMEM((2, 1024, 128), jnp.float32)
         return tuple(
             pl.pallas_call(
                 kernel,
@@ -385,8 +425,9 @@
                 out_specs=[vmem, vmem],
                 scratch_shapes=[pltpu.VMEM(a.shape, a.dtype) for a in arrays]
                 + [tile, tile, wide, wide, wide, wide, tile, tile]
-                + [pltpu.SemaphoreType.DMA((len(arrays),)), pltpu.SemaphoreType.DMA((4,))]
-                + [pltpu.SemaphoreType.DMA((4,)), pltpu.SemaphoreType.REGULAR],
+                + [pltpu.VMEM((2, 6, 64, 128), jnp.float32), pltpu.VMEM((4, 128, 128), jnp.float32)]
+                + [pltpu.SemaphoreType.DMA((len(arrays),)), pltpu.SemaphoreType.DMA((4, 2))]
+                + [pltpu.SemaphoreType.DMA((4, 2)), pltpu.SemaphoreType.REGULAR],
                 compiler_params=pltpu.CompilerParams(collective_id=0, has_side_effects=True),
             )(moduli, mean_strain, *arrays)
         )

time: 40.8 us -> 38.3 us (0.939)
  Pallas kernels: 38.5 us -> 35.8 us
    pallas_call x1, Pallas kernels: 38.5 us -> 35.8 us  [shards(): pl.pallas_call(kernel, out_shape=[pltpu.VMEM(strain.shape, jnp.float32)]...]
where the time goes in v2:
time: 38.3 us; the launch traced here: 37.9 us
  Pallas kernels  35.8 us (93%)
  local copies, waits for them, and re-layouts  1.49 us (4%)
  between operations  0.64 us (2%)
    pallas_call x1, Pallas kernels, shards(): pl.pallas_call(kernel, out_shape=[pltpu.VMEM(strain.shape, jnp.float32)]...  35.8 us
    unnamed x2, local copies, waits for them, and re-layouts  1.49 us

profile of v2, /device:TPU:1, one launch (start us, length us, event | category | flops | bytes accessed | tf_op | source)
XLA Modules:
  0.0 37.9 jit_solution(4085255665630050892)
XLA Ops:
  0.6 35.8 %shard_map.122 = (f32[6,2,64,128]{3,2,1,0:T(8,128)S(1)}, f32[6,2,64,128]{3,2,1,0:T(8,128)S(1)}) custom-call(f32[5]{0:T(128)} %moduli.1, f32[6]{0:T(128)} %mean.1, f32[6,2,64,128]{3,2,1,0:T(8,128)} %strain_hbm.1, s32[2,64,128]{2,1,0:T(8,128)} %labels_hbm.1, s32[2,4,8]{2,1,0:T(4,128)} %normals_hbm.1, bf16[128,768]{1,0:T(8,128)(2,1)} %constant.12.clone.left_hbm, ...), custom_call_target="tpu_custom_call" | custom-call | tf_op jit(solution)/shard_map/pallas_call | solution.py:421
  36.4 0.7 %copy.15 = f32[6,2,64,128]{3,2,1,0:T(8,128)} copy(f32[6,2,64,128]{3,2,1,0:T(8,128)S(1)} %get-tuple-element.2) | data formatting | bytes 786432
  37.2 0.7 %copy.16 = f32[6,2,64,128]{3,2,1,0:T(8,128)} copy(f32[6,2,64,128]{3,2,1,0:T(8,128)S(1)} %get-tuple-element.3) | data formatting | bytes 786432

commit v3 on v2

--- a/solution.py
+++ b/solution.py
@@ -11,6 +11,7 @@
 
 ANGLES = 8
 BLK = 16
+PARTS = 1
 COMPS = (0, 2, 4, 3, 5)
 GROUPS = ((0, 3), (3, 2))
 MESH = pl.DeviceIdType.MESH
@@ -241,9 +242,10 @@
     moduli, mean, strain_hbm, labels_hbm, normals_hbm, left_hbm, right_hbm, fwd_hbm, inv_hbm, twz_hbm, twx_hbm,
     strain_out, stress_out,
     strain, labels, normals, left_ref, right_ref, fwd_ref, inv_ref, twz_ref, twx_ref,
-    s1, r1, s2, r2, s3, r3, s4, r4, cells, maps,
-    load, send, recv, ready,
+    *rest,
 ):
+    s1, r1, s2, r2, s3, r3, s4, r4 = (rest[2 * k : 2 * k + 2] for k in range(8))
+    cells, maps, load, send, recv, ready = rest[16:]
     zs, xs = lax.axis_size("gz"), lax.axis_size("gx")
     total = zs * xs
     j = lax.axis_index("gz")
@@ -262,7 +264,17 @@
         return pz[dz] + high[dy], px[dx] + low[dy] + pc[dc]
 
     z_peers = [peer(0, dy, dz, 0) for dz, dy in far_first((4, 3), (ring, ring)) if dy != 1]
+    early_first = [k + (k - j + zs) // zs for k in range(zs - 1)]
     everyone = far_first((4, 4, 4, 2), (ring, ring, ring, lambda v: 0))
+
+    row = 2 * x + lax.rem(y, 2)
+    early_rows = []
+    for k, (rx, ry) in enumerate(sorted(itertools.product(range(4), range(2)), key=sum)):
+        for dz, dy, dc in far_first((4, 2, 2), (ring, lambda v: 2 * v, lambda v: 0)):
+            early_rows.append((pz[dz] + lax.rem(y // 2 + dy, 2), 4 * rx + 2 * ry + pc[dc]))
+        if k < 7:
+            other = k + (k - row + 8) // 8
+            early_rows.append((j, 2 * other + core))
 
     def x_index(dx, dy, dc):
         low = lax.rem(i // 2 + dy, 2)
@@ -298,7 +310,7 @@
         pol = law(e, lam - lame_ref, 2.0 * (mu - shear_ref), stiff, angle)
         for slot, c in enumerate(COMPS):
             for g in range(8):
-                s1[g, 2 * slot + s] = pol[c][8 * g : 8 * g + 8, :]
+                s1[slot // 3][g, 2 * (slot % 3) + s] = pol[c][8 * g : 8 * g + 8, :]
         for k, value in enumerate((lam, 2.0 * mu, stiff, *angle)):
             cells[s, k] = value
 
@@ -306,45 +318,43 @@
     for to in x_peers:
         pl.semaphore_signal(ready, inc=1, device_id={"gz": j, "gx": to}, device_id_type=MESH)
 
-    def z_send(src, dst, n, g):
-        part = pl.ds(2 * GROUPS[g][0], 2 * GROUPS[g][1])
-        for to, _ in z_peers:
+    def z_send(src, dst, n, g, peers):
+        for to in peers:
             pltpu.make_async_remote_copy(
-                src_ref=src.at[to, part], dst_ref=dst.at[j, part], send_sem=send.at[n, g], recv_sem=recv.at[n, g],
+                src_ref=src[g].at[to], dst_ref=dst[g].at[j], send_sem=send.at[n, g], recv_sem=recv.at[n, g],
                 device_id={"gz": to, "gx": i}, device_id_type=MESH,
             ).start()
-        dst[j, part] = src[j, part]
+        dst[g][j] = src[g][j]
 
     def z_wait(ref, sem, n, g):
-        part = ref.at[pl.ds(0, zs - 1), pl.ds(2 * GROUPS[g][0], 2 * GROUPS[g][1])]
+        part = ref[g].at[pl.ds(0, zs - 1)]
         pltpu.make_async_copy(part, part, sem.at[n, g]).wait()
 
-    def all_send(src, dst, n, g):
+    def all_send(src, dst, n, g, peers):
         mine = pl.multiple_of(me * 8, 8)
         size = GROUPS[g][1]
-        for o in everyone:
-            tz, tx = peer(*o)
+        for tz, tx in peers:
             there = pl.multiple_of((zs * tx + tz) * 8, 8)
             pltpu.make_async_remote_copy(
-                src_ref=src.at[g, pl.ds(there, size), :], dst_ref=dst.at[g, pl.ds(mine, size), :],
+                src_ref=src[g].at[pl.ds(there, size), :], dst_ref=dst[g].at[pl.ds(mine, size), :],
                 send_sem=send.at[n, g], recv_sem=recv.at[n, g],
                 device_id={"gz": tz, "gx": tx}, device_id_type=MESH,
             ).start()
-        dst[g, pl.ds(mine, 8), :] = src[g, pl.ds(mine, 8), :]
+        dst[g][pl.ds(mine, 8), :] = src[g][pl.ds(mine, 8), :]
 
     def all_wait(ref, sem, n, g):
-        part = ref.at[g, pl.ds(0, GROUPS[g][1] * (total - 1)), :]
+        part = ref[g].at[pl.ds(0, GROUPS[g][1] * (total - 1)), :]
         pltpu.make_async_copy(part, part, sem.at[n, g]).wait()
 
     def gathered(ref, g):
-        return [ref[g, pl.ds(c, 128, stride=8), :] for c in range(GROUPS[g][1])]
+        return [ref[g][pl.ds(c, 128, stride=8), :] for c in range(GROUPS[g][1])]
 
     def scatter(ref, g, value):
         for c in range(GROUPS[g][1]):
-            ref[g, pl.ds(c, 128, stride=8), :] = value[:, 128 * c : 128 * c + 128]
-
-    for g in range(2):
-        z_send(s1, r1, 0, g)
+            ref[g][pl.ds(c, 128, stride=8), :] = value[:, 128 * c : 128 * c + 128]
+
+    for g in range(2):
+        z_send(s1, r1, 0, g, [to for to, _ in z_peers])
     scale = -1.0 / (1024.0 * 1024.0)
     half = scale * 0.5 / shear_ref
     couple = scale * (lame_ref + shear_ref) / (shear_ref * (lame_ref + 2.0 * shear_ref))
@@ -356,31 +366,38 @@
     def table(ref):
         return ref[...]
 
-    for g, (first, size) in enumerate(GROUPS):
-        z_wait(r1, recv, 0, g)
-        block = z_forward(lambda a, b: r1[a, b], table(twz_ref), range(first, first + size))
+    def forward(g):
+        block = z_forward(lambda a, b: r1[g][a, b], table(twz_ref), range(GROUPS[g][1]))
         scatter(s2, g, mul(table(left_ref), split3(block, 1), 1, 1))
-        if g == 0:
-            pl.semaphore_wait(ready, xs - 1)
-        all_send(s2, r2, 1, g)
-
-    for g in range(2):
-        all_wait(r2, recv, 1, g)
+
+    def across(g):
         tabs = [table(ref) for ref in (left_ref, right_ref, fwd_ref, inv_ref, twz_ref, twx_ref)]
         wide = jnp.concatenate(gathered(r2, g), axis=1)
         scatter(s3, g, middle(wide, [maps[k] for k in range(4)], half, couple, tabs))
-        all_send(s3, r3, 2, g)
-
-    for g, (first, size) in enumerate(GROUPS):
-        all_wait(r3, recv, 2, g)
+
+    def backward(g):
         flat = jnp.concatenate([w.T for w in gathered(r3, g)], axis=0)
         parts = mul(split3(flat, 1), table(right_ref))
-        for c in range(size):
+        for c in range(GROUPS[g][1]):
             tiles = z_inverse(parts[128 * c : 128 * c + 128], table(twz_ref))
             for k in range(8):
-                s4[k, 2 * (first + c)] = tiles[k][0]
-                s4[k, 2 * (first + c) + 1] = tiles[k][1]
-        z_send(s4, r4, 3, g)
+                s4[g][k, 2 * c] = tiles[k][0]
+                s4[g][k, 2 * c + 1] = tiles[k][1]
+
+    for g in range(2):
+        z_wait(r1, recv, 0, g)
+        forward(g)
+        if g == 0:
+            pl.semaphore_wait(ready, xs - 1)
+        all_send(s2, r2, 1, g, [peer(*o) for o in everyone])
+    for g in range(2):
+        all_wait(r2, recv, 1, g)
+        across(g)
+        all_send(s3, r3, 2, g, early_rows)
+    for g in range(2):
+        all_wait(r3, recv, 2, g)
+        backward(g)
+        z_send(s4, r4, 3, g, early_first)
 
     for g in range(2):
         z_wait(s1, send, 0, g)
@@ -388,7 +405,7 @@
         all_wait(s3, send, 2, g)
 
     def arrived(slot, s):
-        return jnp.concatenate([r4[k, 2 * slot + s] for k in range(8)], axis=0) + mean[COMPS[slot]]
+        return jnp.concatenate([r4[slot // 3][k, 2 * (slot % 3) + s] for k in range(8)], axis=0) + mean[COMPS[slot]]
 
     for g, (first, size) in enumerate(GROUPS):
         z_wait(r4, recv, 3, g)
@@ -407,6 +424,19 @@
         z_wait(s4, send, 3, g)
 
 
+def put_out(strain, stress, strain_hbm, stress_hbm, sem):
+    copies = []
+    size = 6 // PARTS
+    for k in range(PARTS):
+        part = pl.ds(size * k, size)
+        for n, (src, dst) in enumerate(((strain, strain_hbm), (stress, stress_hbm))):
+            copies.append(pltpu.make_async_copy(src.at[part], dst.at[part], sem.at[n, k]))
+    for copy in copies:
+        copy.start()
+    for copy in copies:
+        copy.wait()
+
+
 def solution(mesh):
     consts = tables()
 
@@ -415,21 +445,28 @@
         smem = pl.BlockSpec(memory_space=pltpu.SMEM)
         away = pl.BlockSpec(memory_space=pl.ANY)
         arrays = [strain, labels, normals] + [jnp.asarray(a) for a in consts]
-        tile = pltpu.VMEM((8, 10, 8, 128), jnp.float32)
-        wide = pltpu.VMEM((2, 1024, 128), jnp.float32)
+        tiles = [pltpu.VMEM((8, 2 * n, 8, 128), jnp.float32) for _, n in GROUPS]
+        wide = [pltpu.VMEM((1024, 128), jnp.float32)] * 2
+        fields = pl.pallas_call(
+            kernel,
+            out_shape=[pltpu.VMEM(strain.shape, jnp.float32)] * 2,
+            in_specs=[smem, smem] + [away] * len(arrays),
+            out_specs=[vmem, vmem],
+            scratch_shapes=[pltpu.VMEM(a.shape, a.dtype) for a in arrays]
+            + tiles * 2 + wide * 4 + tiles * 2
+            + [pltpu.VMEM((2, 6, 64, 128), jnp.float32), pltpu.VMEM((4, 128, 128), jnp.float32)]
+            + [pltpu.SemaphoreType.DMA((len(arrays),)), pltpu.SemaphoreType.DMA((4, 2))]
+            + [pltpu.SemaphoreType.DMA((4, 2)), pltpu.SemaphoreType.REGULAR],
+            compiler_params=pltpu.CompilerParams(collective_id=0, has_side_effects=True),
+        )(moduli, mean_strain, *arrays)
         return tuple(
             pl.pallas_call(
-                kernel,
-                out_shape=[pltpu.VMEM(strain.shape, jnp.float32)] * 2,
-                in_specs=[smem, smem] + [away] * len(arrays),
-                out_specs=[vmem, vmem],
-                scratch_shapes=[pltpu.VMEM(a.shape, a.dtype) for a in arrays]
-                + [tile, tile, wide, wide, wide, wide, tile, tile]
-                + [pltpu.VMEM((2, 6, 64, 128), jnp.float32), pltpu.VMEM((4, 128, 128), jnp.float32)]
-                + [pltpu.SemaphoreType.DMA((len(arrays),)), pltpu.SemaphoreType.DMA((4, 2))]
-                + [pltpu.SemaphoreType.DMA((4, 2)), pltpu.SemaphoreType.REGULAR],
-                compiler_params=pltpu.CompilerParams(collective_id=0, has_side_effects=True),
-            )(moduli, mean_strain, *arrays)
+                put_out,
+                out_shape=[jax.ShapeDtypeStruct(strain.shape, jnp.float32)] * 2,
+                in_specs=[vmem] * 2,
+                out_specs=[away] * 2,
+                scratch_shapes=[pltpu.SemaphoreType.DMA((2, PARTS))],
+            )(*[pltpu.with_memory_space_constraint(a, pltpu.VMEM) for a in fields])
         )
 
     in_specs = (P(None, None, "gx", "gz"), P(None, "gx", "gz"), P(None, "gx", "gz"), P(), P())

time: 38.3 us -> 37.3 us (0.974)
  local copies, waits for them, and re-layouts: 1.49 us -> 0 us
  Pallas kernels: 35.8 us -> 36.6 us
    unnamed x2 -> x0, local copies, waits for them, and re-layouts: 1.49 us -> none
    pallas_call x0 -> x1, Pallas kernels: none -> 0.89 us  [shards(): pl.pallas_call(put_out, out_shape=[jax.ShapeDtypeStruct(strain.shape, jnp...]
where the time goes in v3:
time: 37.3 us; the launch traced here: 37.2 us
  Pallas kernels  36.6 us (98%)
  between operations  0.64 us (2%)
    pallas_call x1, Pallas kernels, shards(): pl.pallas_call(kernel, out_shape=[pltpu.VMEM(strain.shape, jnp.float32)]...  35.7 us
    pallas_call x1, Pallas kernels, shards(): pl.pallas_call(put_out, out_shape=[jax.ShapeDtypeStruct(strain.shape, jnp...  0.89 us

profile of v3, /device:TPU:1, one launch (start us, length us, event | category | flops | bytes accessed | tf_op | source)
XLA Modules:
  0.0 37.2 jit_solution(16464623584984696882)
XLA Ops:
  0.6 35.7 %shard_map.122 = (f32[6,2,64,128]{3,2,1,0:T(8,128)S(1)}, f32[6,2,64,128]{3,2,1,0:T(8,128)S(1)}) custom-call(f32[5]{0:T(128)} %moduli.1, f32[6]{0:T(128)} %mean.1, f32[6,2,64,128]{3,2,1,0:T(8,128)} %strain_hbm.1, s32[2,64,128]{2,1,0:T(8,128)} %labels_hbm.1, s32[2,4,8]{2,1,0:T(4,128)} %normals_hbm.1, bf16[128,768]{1,0:T(8,128)(2,1)} %constant.12.clone.left_hbm, ...), custom_call_target="tpu_custom_call" | custom-call | tf_op jit(solution)/shard_map/pallas_call | solution.py:450
  36.3 0.9 %shard_map.123 = (f32[6,2,64,128]{3,2,1,0:T(8,128)}, f32[6,2,64,128]{3,2,1,0:T(8,128)}) custom-call(f32[6,2,64,128]{3,2,1,0:T(8,128)S(1)} %get-tuple-element.4.strain, f32[6,2,64,128]{3,2,1,0:T(8,128)S(1)} %get-tuple-element.5.stress), custom_call_target="tpu_custom_call" | custom-call | tf_op jit(solution)/shard_map/pallas_call | solution.py:463

commit v4 on v3

--- a/solution.py
+++ b/solution.py
@@ -239,9 +239,9 @@
 
 
 def kernel(
-    moduli, mean, strain_hbm, labels_hbm, normals_hbm, left_hbm, right_hbm, fwd_hbm, inv_hbm, twz_hbm, twx_hbm,
+    strain_hbm, labels_hbm, normals_hbm, moduli_hbm, mean_hbm, left_hbm, right_hbm, fwd_hbm, inv_hbm, twz_hbm, twx_hbm,
     strain_out, stress_out,
-    strain, labels, normals, left_ref, right_ref, fwd_ref, inv_ref, twz_ref, twx_ref,
+    strain, labels, normals, moduli, mean, left_ref, right_ref, fwd_ref, inv_ref, twz_ref, twx_ref,
     *rest,
 ):
     s1, r1, s2, r2, s3, r3, s4, r4 = (rest[2 * k : 2 * k + 2] for k in range(8))
@@ -250,6 +250,22 @@
     total = zs * xs
     j = lax.axis_index("gz")
     i = lax.axis_index("gx")
+    barrier = pltpu.get_barrier_semaphore()
+    for k in (5, 3, 4, 1, 7, 2, 6):
+        pl.semaphore_signal(barrier, inc=1, device_id={"gz": lax.rem(j + k, zs), "gx": i}, device_id_type=MESH)
+    for k in (10, 6, 8, 11, 9, 7, 5, 12, 4, 13, 3, 14, 2, 15, 1):
+        pl.semaphore_signal(barrier, inc=1, device_id={"gz": j, "gx": lax.rem(i + k, xs)}, device_id_type=MESH)
+
+    loads = [
+        pltpu.make_async_copy(a, b, load.at[k])
+        for k, (a, b) in enumerate((
+            (strain_hbm, strain), (labels_hbm, labels), (normals_hbm, normals), (moduli_hbm, moduli),
+            (mean_hbm, mean), (twz_hbm, twz_ref),
+            (left_hbm, left_ref), (twx_hbm, twx_ref), (fwd_hbm, fwd_ref), (inv_hbm, inv_ref), (right_hbm, right_ref),
+        ))
+    ]
+    for copy in loads:
+        copy.start()
     me = zs * i + j
     z, x, core = j // 2, i // 4, lax.rem(i, 2)
     y = 2 * lax.rem(j, 2) + lax.rem(i // 2, 2)
@@ -282,22 +298,7 @@
 
     x_peers = [x_index(*o) for o in far_first((4, 2, 2), (ring, lambda v: v, lambda v: 0))]
 
-    barrier = pltpu.get_barrier_semaphore()
-    for to, _ in z_peers:
-        pl.semaphore_signal(barrier, inc=1, device_id={"gz": to, "gx": i}, device_id_type=MESH)
-    for to in x_peers:
-        pl.semaphore_signal(barrier, inc=1, device_id={"gz": j, "gx": to}, device_id_type=MESH)
-
-    loads = [
-        pltpu.make_async_copy(a, b, load.at[k])
-        for k, (a, b) in enumerate((
-            (strain_hbm, strain), (labels_hbm, labels), (normals_hbm, normals), (twz_hbm, twz_ref),
-            (left_hbm, left_ref), (twx_hbm, twx_ref), (fwd_hbm, fwd_ref), (inv_hbm, inv_ref), (right_hbm, right_ref),
-        ))
-    ]
-    for copy in loads:
-        copy.start()
-    for copy in loads[:3]:
+    for copy in loads[:5]:
         copy.wait()
 
     m = [moduli[k] for k in range(5)]
@@ -360,7 +361,7 @@
     couple = scale * (lame_ref + shear_ref) / (shear_ref * (lame_ref + 2.0 * shear_ref))
     for k, value in enumerate(green_maps(8 * me)):
         maps[k] = value
-    for copy in loads[3:]:
+    for copy in loads[5:]:
         copy.wait()
 
     def table(ref):
@@ -442,23 +443,22 @@
 
     def shards(strain, labels, normals, moduli, mean_strain):
         vmem = pl.BlockSpec(memory_space=pltpu.VMEM)
-        smem = pl.BlockSpec(memory_space=pltpu.SMEM)
         away = pl.BlockSpec(memory_space=pl.ANY)
-        arrays = [strain, labels, normals] + [jnp.asarray(a) for a in consts]
+        arrays = [strain, labels, normals, moduli, mean_strain] + [jnp.asarray(a) for a in consts]
         tiles = [pltpu.VMEM((8, 2 * n, 8, 128), jnp.float32) for _, n in GROUPS]
         wide = [pltpu.VMEM((1024, 128), jnp.float32)] * 2
         fields = pl.pallas_call(
             kernel,
             out_shape=[pltpu.VMEM(strain.shape, jnp.float32)] * 2,
-            in_specs=[smem, smem] + [away] * len(arrays),
+            in_specs=[away] * len(arrays),
             out_specs=[vmem, vmem],
-            scratch_shapes=[pltpu.VMEM(a.shape, a.dtype) for a in arrays]
+            scratch_shapes=[(pltpu.SMEM if a.ndim == 1 else pltpu.VMEM)(a.shape, a.dtype) for a in arrays]
             + tiles * 2 + wide * 4 + tiles * 2
             + [pltpu.VMEM((2, 6, 64, 128), jnp.float32), pltpu.VMEM((4, 128, 128), jnp.float32)]
             + [pltpu.SemaphoreType.DMA((len(arrays),)), pltpu.SemaphoreType.DMA((4, 2))]
             + [pltpu.SemaphoreType.DMA((4, 2)), pltpu.SemaphoreType.REGULAR],
             compiler_params=pltpu.CompilerParams(collective_id=0, has_side_effects=True),
-        )(moduli, mean_strain, *arrays)
+        )(*arrays)
         return tuple(
             pl.pallas_call(
                 put_out,

time: 37.3 us -> 36.6 us (0.981)
  Pallas kernels: 36.6 us -> 35.8 us
    pallas_call x1, Pallas kernels: 35.7 us -> 34.9 us  [shards(): pl.pallas_call(kernel, out_shape=[pltpu.VMEM(strain.shape, jnp.float32)]...]
where the time goes in v4:
time: 36.6 us; the launch traced here: 36.5 us
  Pallas kernels  35.8 us (98%)
  between operations  0.64 us (2%)
    pallas_call x1, Pallas kernels, shards(): pl.pallas_call(kernel, out_shape=[pltpu.VMEM(strain.shape, jnp.float32)]...  34.9 us
    pallas_call x1, Pallas kernels, shards(): pl.pallas_call(put_out, out_shape=[jax.ShapeDtypeStruct(strain.shape, jnp...  0.89 us

profile of v4, /device:TPU:1, one launch (start us, length us, event | category | flops | bytes accessed | tf_op | source)
XLA Modules:
  0.0 36.5 jit_solution(9944140658500333170)
XLA Ops:
  0.6 34.9 %shard_map.122 = (f32[6,2,64,128]{3,2,1,0:T(8,128)S(1)}, f32[6,2,64,128]{3,2,1,0:T(8,128)S(1)}) custom-call(f32[6,2,64,128]{3,2,1,0:T(8,128)} %strain_hbm.1, s32[2,64,128]{2,1,0:T(8,128)} %labels_hbm.1, s32[2,4,8]{2,1,0:T(4,128)} %normals_hbm.1, f32[5]{0:T(128)} %moduli_hbm.1, f32[6]{0:T(128)} %mean_hbm.1, bf16[128,768]{1,0:T(8,128)(2,1)} %constant.12.clone.left_hbm, ...), custom_call_target="tpu_custom_call" | custom-call | tf_op jit(solution)/shard_map/pallas_call | solution.py:450
  35.6 0.9 %shard_map.123 = (f32[6,2,64,128]{3,2,1,0:T(8,128)}, f32[6,2,64,128]{3,2,1,0:T(8,128)}) custom-call(f32[6,2,64,128]{3,2,1,0:T(8,128)S(1)} %get-tuple-element.4.strain, f32[6,2,64,128]{3,2,1,0:T(8,128)S(1)} %get-tuple-element.5.stress), custom_call_target="tpu_custom_call" | custom-call | tf_op jit(solution)/shard_map/pallas_call | solution.py:463

commit v5 on v4

--- a/solution.py
+++ b/solution.py
@@ -40,7 +40,8 @@
     fwd2 = np.concatenate([fwd, np.roll(fwd, 64, axis=0)], axis=0)
     inv2 = np.concatenate([inv, np.roll(inv, 64, axis=1)], axis=1)
     twz, twx = np.asarray(twz, np.float32), np.asarray(twx, np.float32)
-    return [left_table(dft), right_table(dft), right_table(fwd2), right_table(inv2), twz, twx]
+    stacked = np.concatenate([np.cos(w), np.sin(w)], axis=0)
+    return [left_table(dft), right_table(dft), right_table(fwd2), right_table(inv2), twz, twx, left_table(stacked)]
 
 
 def halves(a):
@@ -164,7 +165,7 @@
 
 
 def middle(wide, maps, half, couple, tabs):
-    left, _, fwd, inv, _, twx = tabs
+    left, _, fwd, inv, _, twx, both_left = tabs
     n = wide.shape[1] // 128
     lane = lax.broadcasted_iota(jnp.int32, (128, 128), 1)
     sign = jnp.where(lane < 64, 1.0, -1.0)
@@ -176,9 +177,11 @@
     def rows(x, c):
         return x[128 * c : 128 * c + 128]
 
-    pairs = [jnp.concatenate([lanes(wide, c), swap(lanes(wide, c)) * sign], axis=0) for c in range(n)]
-    x1 = mul(left, split3(jnp.concatenate(pairs, axis=1), 0))
-    turned = [jnp.concatenate([lanes(x1, c) * cx, -(lanes(x1, c) * sx)], axis=1) for c in range(n)]
+    cs = mul(both_left, split3(wide, 0))
+    turned = []
+    for c in range(n):
+        v, u = lanes(cs[:128], c), -(lanes(cs[128:], c) * sign)
+        turned.append(jnp.concatenate([v * cx + u * sx, u * cx - v * sx], axis=1))
     spec = mul(split3(jnp.concatenate(turned, axis=0), 1), fwd)
     new = green([rows(spec, c) for c in range(n)], maps, half, couple)
     both = mul(split3(jnp.concatenate(new, axis=0), 1), inv)
@@ -187,10 +190,6 @@
         y, ry = rows(both, c)[:, :128], rows(both, c)[:, 128:]
         out.append(jnp.concatenate([y * cx - ry * sx, -((ry * cx + y * sx) * sign)], axis=0))
     return mul(left, split3(jnp.concatenate(out, axis=1), 0))
-
-
-def swap(x):
-    return pltpu.roll(x, 64, axis=1)
 
 
 def stress_terms(moduli, labels):
@@ -239,9 +238,9 @@
 
 
 def kernel(
-    strain_hbm, labels_hbm, normals_hbm, moduli_hbm, mean_hbm, left_hbm, right_hbm, fwd_hbm, inv_hbm, twz_hbm, twx_hbm,
+    strain_hbm, labels_hbm, normals_hbm, moduli_hbm, mean_hbm, left_hbm, right_hbm, fwd_hbm, inv_hbm, twz_hbm, twx_hbm, both_hbm,
     strain_out, stress_out,
-    strain, labels, normals, moduli, mean, left_ref, right_ref, fwd_ref, inv_ref, twz_ref, twx_ref,
+    strain, labels, normals, moduli, mean, left_ref, right_ref, fwd_ref, inv_ref, twz_ref, twx_ref, both_ref,
     *rest,
 ):
     s1, r1, s2, r2, s3, r3, s4, r4 = (rest[2 * k : 2 * k + 2] for k in range(8))
@@ -262,6 +261,7 @@
             (strain_hbm, strain), (labels_hbm, labels), (normals_hbm, normals), (moduli_hbm, moduli),
             (mean_hbm, mean), (twz_hbm, twz_ref),
             (left_hbm, left_ref), (twx_hbm, twx_ref), (fwd_hbm, fwd_ref), (inv_hbm, inv_ref), (right_hbm, right_ref),
+            (both_hbm, both_ref),
         ))
     ]
     for copy in loads:
@@ -285,7 +285,7 @@
 
     row = 2 * x + lax.rem(y, 2)
     early_rows = []
-    for k, (rx, ry) in enumerate(sorted(itertools.product(range(4), range(2)), key=sum)):
+    for k, (rx, ry) in enumerate(itertools.product(range(4), range(2))):
         for dz, dy, dc in far_first((4, 2, 2), (ring, lambda v: 2 * v, lambda v: 0)):
             early_rows.append((pz[dz] + lax.rem(y // 2 + dy, 2), 4 * rx + 2 * ry + pc[dc]))
         if k < 7:
@@ -316,8 +316,6 @@
             cells[s, k] = value
 
     pl.semaphore_wait(barrier, zs + xs - 2)
-    for to in x_peers:
-        pl.semaphore_signal(ready, inc=1, device_id={"gz": j, "gx": to}, device_id_type=MESH)
 
     def z_send(src, dst, n, g, peers):
         for to in peers:
@@ -325,7 +323,6 @@
                 src_ref=src[g].at[to], dst_ref=dst[g].at[j], send_sem=send.at[n, g], recv_sem=recv.at[n, g],
                 device_id={"gz": to, "gx": i}, device_id_type=MESH,
             ).start()
-        dst[g][j] = src[g][j]
 
     def z_wait(ref, sem, n, g):
         part = ref[g].at[pl.ds(0, zs - 1)]
@@ -356,6 +353,10 @@
 
     for g in range(2):
         z_send(s1, r1, 0, g, [to for to, _ in z_peers])
+    for g in range(2):
+        r1[g][j] = s1[g][j]
+    for to in x_peers:
+        pl.semaphore_signal(ready, inc=1, device_id={"gz": j, "gx": to}, device_id_type=MESH)
     scale = -1.0 / (1024.0 * 1024.0)
     half = scale * 0.5 / shear_ref
     couple = scale * (lame_ref + shear_ref) / (shear_ref * (lame_ref + 2.0 * shear_ref))
@@ -372,7 +373,7 @@
         scatter(s2, g, mul(table(left_ref), split3(block, 1), 1, 1))
 
     def across(g):
-        tabs = [table(ref) for ref in (left_ref, right_ref, fwd_ref, inv_ref, twz_ref, twx_ref)]
+        tabs = [table(ref) for ref in (left_ref, right_ref, fwd_ref, inv_ref, twz_ref, twx_ref, both_ref)]
         wide = jnp.concatenate(gathered(r2, g), axis=1)
         scatter(s3, g, middle(wide, [maps[k] for k in range(4)], half, couple, tabs))
 
@@ -399,6 +400,7 @@
         all_wait(r3, recv, 2, g)
         backward(g)
         z_send(s4, r4, 3, g, early_first)
+        r4[g][j] = s4[g][j]
 
     for g in range(2):
         z_wait(s1, send, 0, g)

time: 36.6 us -> 36.6 us (level)
  no operation moved by 1% of the time
where the time goes in v5:
time: 36.6 us; the launch traced here: 36.4 us
  Pallas kernels  35.8 us (98%)
  between operations  0.64 us (2%)
    pallas_call x1, Pallas kernels, shards(): pl.pallas_call(kernel, out_shape=[pltpu.VMEM(strain.shape, jnp.float32)]...  34.9 us
    pallas_call x1, Pallas kernels, shards(): pl.pallas_call(put_out, out_shape=[jax.ShapeDtypeStruct(strain.shape, jnp...  0.89 us

profile of v5, /device:TPU:1, one launch (start us, length us, event | category | flops | bytes accessed | tf_op | source)
XLA Modules:
  0.0 36.4 jit_solution(9444316483128280964)
XLA Ops:
  0.6 34.9 %shard_map.131 = (f32[6,2,64,128]{3,2,1,0:T(8,128)S(1)}, f32[6,2,64,128]{3,2,1,0:T(8,128)S(1)}) custom-call(f32[6,2,64,128]{3,2,1,0:T(8,128)} %strain_hbm.1, s32[2,64,128]{2,1,0:T(8,128)} %labels_hbm.1, s32[2,4,8]{2,1,0:T(4,128)} %normals_hbm.1, f32[5]{0:T(128)} %moduli_hbm.1, f32[6]{0:T(128)} %mean_hbm.1, bf16[128,768]{1,0:T(8,128)(2,1)} %constant.14.clone.left_hbm, ...), custom_call_target="tpu_custom_call" | custom-call | tf_op jit(solution)/shard_map/pallas_call | solution.py:452
  35.5 0.9 %shard_map.132 = (f32[6,2,64,128]{3,2,1,0:T(8,128)}, f32[6,2,64,128]{3,2,1,0:T(8,128)}) custom-call(f32[6,2,64,128]{3,2,1,0:T(8,128)S(1)} %get-tuple-element.4.strain, f32[6,2,64,128]{3,2,1,0:T(8,128)S(1)} %get-tuple-element.5.stress), custom_call_target="tpu_custom_call" | custom-call | tf_op jit(solution)/shard_map/pallas_call | solution.py:465

commit v6 on v5

--- a/solution.py
+++ b/solution.py
@@ -246,6 +246,7 @@
     s1, r1, s2, r2, s3, r3, s4, r4 = (rest[2 * k : 2 * k + 2] for k in range(8))
     cells, maps, load, send, recv, ready = rest[16:]
     zs, xs = lax.axis_size("gz"), lax.axis_size("gx")
+    zs_stride = xs
     total = zs * xs
     j = lax.axis_index("gz")
     i = lax.axis_index("gx")
@@ -283,14 +284,25 @@
     early_first = [k + (k - j + zs) // zs for k in range(zs - 1)]
     everyone = far_first((4, 4, 4, 2), (ring, ring, ring, lambda v: 0))
 
+    def named(tz, tx):
+        return zs_stride * tz + tx, 8 * (zs * tx + tz)
+
+    columns = {(dx, dy): named(high[dy], px[dx] + low[dy]) for dx in range(4) for dy in range(4)}
+    stacks = {(dz, dc): named(pz[dz], pc[dc]) for dz in range(4) for dc in range(2)}
+
+    def both(a, b):
+        return a[0] + b[0], a[1] + b[1]
+
+    everyone = [both(columns[o[:2]], stacks[o[2:]]) for o in everyone]
+
     row = 2 * x + lax.rem(y, 2)
     early_rows = []
     for k, (rx, ry) in enumerate(itertools.product(range(4), range(2))):
         for dz, dy, dc in far_first((4, 2, 2), (ring, lambda v: 2 * v, lambda v: 0)):
-            early_rows.append((pz[dz] + lax.rem(y // 2 + dy, 2), 4 * rx + 2 * ry + pc[dc]))
+            early_rows.append(both(named(lax.rem(y // 2 + dy, 2), 4 * rx + 2 * ry), stacks[dz, dc]))
         if k < 7:
             other = k + (k - row + 8) // 8
-            early_rows.append((j, 2 * other + core))
+            early_rows.append(named(j, 2 * other + core))
 
     def x_index(dx, dy, dc):
         low = lax.rem(i // 2 + dy, 2)
@@ -331,12 +343,12 @@
     def all_send(src, dst, n, g, peers):
         mine = pl.multiple_of(me * 8, 8)
         size = GROUPS[g][1]
-        for tz, tx in peers:
-            there = pl.multiple_of((zs * tx + tz) * 8, 8)
+        for to, there in peers:
+            there = pl.multiple_of(there, 8)
             pltpu.make_async_remote_copy(
                 src_ref=src[g].at[pl.ds(there, size), :], dst_ref=dst[g].at[pl.ds(mine, size), :],
                 send_sem=send.at[n, g], recv_sem=recv.at[n, g],
-                device_id={"gz": tz, "gx": tx}, device_id_type=MESH,
+                device_id=to, device_id_type=pl.DeviceIdType.LOGICAL,
             ).start()
         dst[g][pl.ds(mine, 8), :] = src[g][pl.ds(mine, 8), :]
 
@@ -391,7 +403,7 @@
         forward(g)
         if g == 0:
             pl.semaphore_wait(ready, xs - 1)
-        all_send(s2, r2, 1, g, [peer(*o) for o in everyone])
+        all_send(s2, r2, 1, g, everyone)
     for g in range(2):
         all_wait(r2, recv, 1, g)
         across(g)

time: 36.6 us -> 36.6 us (level)
  no operation moved by 1% of the time
where the time goes in v6:
time: 36.6 us; the launch traced here: 36.4 us
  Pallas kernels  35.8 us (98%)
  between operations  0.64 us (2%)
    pallas_call x1, Pallas kernels, shards(): pl.pallas_call(kernel, out_shape=[pltpu.VMEM(strain.shape, jnp.float32)]...  34.9 us
    pallas_call x1, Pallas kernels, shards(): pl.pallas_call(put_out, out_shape=[jax.ShapeDtypeStruct(strain.shape, jnp...  0.89 us

profile of v6, /device:TPU:1, one launch (start us, length us, event | category | flops | bytes accessed | tf_op | source)
XLA Modules:
  0.0 36.4 jit_solution(12258623956126349058)
XLA Ops:
  0.6 34.9 %shard_map.131 = (f32[6,2,64,128]{3,2,1,0:T(8,128)S(1)}, f32[6,2,64,128]{3,2,1,0:T(8,128)S(1)}) custom-call(f32[6,2,64,128]{3,2,1,0:T(8,128)} %strain_hbm.1, s32[2,64,128]{2,1,0:T(8,128)} %labels_hbm.1, s32[2,4,8]{2,1,0:T(4,128)} %normals_hbm.1, f32[5]{0:T(128)} %moduli_hbm.1, f32[6]{0:T(128)} %mean_hbm.1, bf16[128,768]{1,0:T(8,128)(2,1)} %constant.14.clone.left_hbm, ...), custom_call_target="tpu_custom_call" | custom-call | tf_op jit(solution)/shard_map/pallas_call | solution.py:464
  35.5 0.9 %shard_map.132 = (f32[6,2,64,128]{3,2,1,0:T(8,128)}, f32[6,2,64,128]{3,2,1,0:T(8,128)}) custom-call(f32[6,2,64,128]{3,2,1,0:T(8,128)S(1)} %get-tuple-element.4.strain, f32[6,2,64,128]{3,2,1,0:T(8,128)S(1)} %get-tuple-element.5.stress), custom_call_target="tpu_custom_call" | custom-call | tf_op jit(solution)/shard_map/pallas_call | solution.py:477
